TPU v7x, 32 devices: a whole 2x2x4 slice. The times are simulated.
32 devices in a mesh: wave: 32 (over z, y, x, core), lev: 1.
Axes of the slice: x: 2, y: 2, z: 4, core: 2. Of those that a mesh axis runs over, the one named last changes fastest.
Arguments:
- grid_adjoint: bfloat16 [3, 4, 128, 1536], P(None, 'lev', 'wave'), may hold values from -6 to 6
- courant: bfloat16 [4, 128, 1536], P('lev', 'wave'), may hold values from -0.8984375 to 0.8984375
- row_points: int32 [128], P('wave'), may hold values from 20 to 1536, as said below
- wave_order: int32 [512], replicated, may hold values from 0 to 511, as said below
- legendre: bfloat16 [512, 512, 128], P('wave', 'lev'), may hold values from -0.013671875 to 0.013671875
- vert_inverse: float32 [3, 4, 4], replicated, as said below
Outputs:
- spectral_adjoint: float32 [3, 4, 512, 2, 512], P(None, None, ('wave', 'lev'))
Inputs may be any that keep to these rules, and one draw needn't show every extreme that they name: Row j has row_points[j] grid points; positions at or beyond it are unused. `wave_order`: A permutation of the wavenumbers 0 to 511 in which slots 2 i and 2 i + 1 hold wavenumbers that sum to 511. `vert_inverse`: each field's matrix has diagonal entries between 0.5 and 2 plus a dense coupling of independent entries.
All inputs are finite; a program needn't handle non-finite values.
Results may differ from a plain program's by a relative error of at most 0.0047.
Values may be sent and summed in bfloat16 or wider, within the bound.
No kernel may reach another device: no remote copies, remote signals or barrier semaphores. Data moves between devices by JAX's collectives and lax.ppermute only.
A program may use at most 64 MiB of HBM per device.

v0:
```python
import math

import jax
import jax.numpy as jnp
from jax import lax
from jax.sharding import PartitionSpec as P

TWO_PI = 2.0 * math.pi


def advect(grid_rows, wind_rows, points):
    row_width = grid_rows.shape[-1]
    positions = jnp.arange(row_width, dtype=jnp.int32)
    counts = points[:, None]
    inside = positions[None, :] < counts
    at_end = positions[None, :] == counts - 1
    mass_flux = jnp.where(
        inside, wind_rows.astype(jnp.float32)[None] * grid_rows.astype(jnp.float32), 0.0
    )
    first_flux = mass_flux[..., :1]
    last_flux = jnp.sum(jnp.where(at_end, mass_flux, 0.0), axis=-1, keepdims=True)
    forward_flux = jnp.where(at_end, first_flux, jnp.roll(mass_flux, -1, axis=-1))
    backward_flux = jnp.where(positions == 0, last_flux, jnp.roll(mass_flux, 1, axis=-1))
    result = jnp.where(
        inside, grid_rows.astype(jnp.float32) + 0.5 * (forward_flux - backward_flux), 0.0
    )
    return result.astype(jnp.bfloat16)


def fourier_table(points, orders, row_width):
    positions = jnp.arange(row_width, dtype=jnp.int32)
    counts = points[:, None, None]
    phase_index = orders[None, None, :] * positions[None, :, None] % counts
    angles = phase_index.astype(jnp.float32) * (TWO_PI / counts.astype(jnp.float32))
    highest = (counts - 1) // 2
    factor = jnp.where(
        orders[None, None, :] > highest, 0.0, jnp.where(orders[None, None, :] == 0, 1.0, 2.0)
    ).astype(jnp.float32)
    cosines = jnp.stack([jnp.cos(angles) * factor, -jnp.sin(angles) * factor], axis=-1)
    return cosines.reshape(points.shape[0], row_width, 2 * orders.shape[0]).astype(jnp.bfloat16)


def body(grid_adjoint, courant, row_points, wave_order, legendre, vert_inverse):
    fields, levels_dev, row_count, row_width = grid_adjoint.shape
    row_group = math.gcd(4, row_count)

    def row_block(start):
        advected = advect(grid_adjoint, courant, row_points)
        cosines = fourier_table(row_points, wave_order, row_width)
        return lax.dot_general(
            advected, cosines, (((3,), (1,)), ((2,), (0,))), preferred_element_type=jnp.float32
        )

    starts = jnp.arange(0, row_count, row_group, dtype=jnp.int32)
    fourier = lax.map(row_block, starts)
    fourier = fourier.reshape(row_count, fields, levels_dev, -1).astype(jnp.bfloat16)
    fourier = jnp.transpose(fourier, (2, 1, 3, 0))
    table_quarter = lax.all_to_all(legendre, "lev", split_axis=0, concat_axis=1, tiled=True)
    spectral = lax.all_to_all(
        lax.all_to_all(fourier, "wave", split_axis=2, concat_axis=3, tiled=True),
        "lev",
        split_axis=2,
        concat_axis=0,
        tiled=True,
    )
    slot_count = table_quarter.shape[0]
    wave_total = table_quarter.shape[1]
    first_slot = (
        lax.axis_index("wave") * lax.axis_size("lev") + lax.axis_index("lev")
    ) * slot_count
    orders = lax.dynamic_slice_in_dim(wave_order, first_slot, slot_count, 0)
    degrees = jnp.arange(wave_total, dtype=jnp.int32)
    masked = jnp.where(
        degrees[None, :, None] >= orders[:, None, None], table_quarter, jnp.zeros((), jnp.bfloat16)
    )
    levels = spectral.shape[0]
    flattened = spectral.reshape(levels * fields, slot_count, 2, spectral.shape[-1])
    partial_value = lax.dot_general(
        flattened, masked, (((3,), (2,)), ((1,), (0,))), preferred_element_type=jnp.float32
    )
    partial_value = partial_value.reshape(slot_count, levels, fields, 2, wave_total)
    return jnp.einsum(
        "fpl,ipfcn->flicn", vert_inverse, partial_value, precision=lax.Precision.HIGHEST
    )


def solution(mesh):
    return jax.shard_map(
        body,
        mesh=mesh,
        in_specs=(
            P(None, "lev", "wave", None),
            P("lev", "wave", None),
            P("wave"),
            P(),
            P("wave", "lev", None),
            P(),
        ),
        out_specs=P(None, None, ("wave", "lev"), None, None),
        check_vma=False,
    )
```

profile of v0, /device:TPU:0, one launch (start us, length us, event | category | flops | bytes accessed | tf_op | source)
XLA Modules:
  0.0 408.1 jit_solution(9162306586121915211)
XLA Ops:
  0.0 0.0 copy-start
  0.0 0.7 broadcast_add_fusion
  0.7 0.7 convert_divide_fusion
  1.3 0.7 broadcast_compare_fusion
  2.0 0.7 compare_select_fusion.2
  2.7 0.9 iota_multiply_fusion
  3.6 0.8 convert_element_type.46
  4.5 0.7 iota_compare_fusion.1
  5.2 1.0 fusion.25
  6.2 0.1 slice_reduce_fusion
  6.3 0.2 fusion.35
  6.5 0.9 compare_select_fusion
  7.4 336.8 %multiply_convert_fusion.1 = (bf16[4,1536,512,1]{1,0,3,2:T(4,128)(2,1)S(1)}, bf16[4,1536,512,1]{1,0,3,2:T(4,128)(2,1)S(1)}) fusion(f32[4,512]{0,1:T(8,128)S(1)} %compare_select_fusion, f32[4]{0:T(128)S(1)} %convert_divide_fusion, pred[4]{0:T(512)(128)(4,1)S(1)} %broadcast_compare_fusion, s32[4]{0:T(128)S(1)} %get-tuple-element.32, ...), kind=kLoop, calls=%fused_computation.11 | loop fusion | flops 44040192 | bytes 15736868 | tf_op jit(solution)/shard_map/convert
  344.2 0.0 copy-start.1
  344.3 8.4 %pad_maximum_fusion = bf16[4,1536,512,2]{1,0,3,2:T(4,128)(2,1)S(1)} fusion(bf16[4,1536,512,1]{1,0,3,2:T(4,128)(2,1)S(1)} %get-tuple-element.16, bf16[4,1536,512,1]{1,0,3,2:T(4,128)(2,1)S(1)} %get-tuple-element.15), kind=kLoop, calls=%fused_computation.7 | loop fusion | flops 6291456 | bytes 25165824 | tf_op jit(solution)/shard_map/while/body/eval_jaxpr/stack | solution.py:39
  352.6 0.0 copy-done.1
  352.6 0.6 fusion.12
  353.3 5.0 %fusion.20 = bf16[4,3,1024,4]{2,0,1,3:T(4,128)(2,1)S(1)} fusion(bf16[4,1536,1024,1]{1,0,2,3:T(4,128)(2,1)S(1)} %bitcast.26, bf16[3,4,4,1536]{3,2,1,0:T(4,128)(2,1)S(1)} %fusion.12), kind=kOutput, calls=%fused_computation.28 | convolution fusion | flops 151044096 | bytes 12828672 | tf_op jit(solution)/shard_map/while/body/eval_jaxpr/dot_general | solution.py:50
  358.2 2.9 copy.31
  361.1 6.9 %reshape.186 = bf16[32,2,768]{2,1,0:T(2,128)(2,1)} reshape(bf16[1024,3,4,4]{3,2,1,0:T(4,128)(2,1)S(1)} %bitcast.27) | data formatting | bytes 196608
  368.0 7.5 %all-to-all-start = ((bf16[32,2,768]{2,1,0:T(2,128)(2,1)}), bf16[32,2,768]{2,1,0:T(2,128)(2,1)S(1)}, u32[]{:S(2)}, u32[]{:S(2)}) async-start(bf16[32,2,768]{2,1,0:T(2,128)(2,1)} %reshape.186), calls=%async_computation | async-start | bytes 196608 | tf_op jit(solution)/shard_map/all_to_all | solution.py:60
  375.5 0.8 dynamic_slice.3
  376.3 0.1 iota_compare_fusion
  376.4 6.9 %all-to-all-done = bf16[32,2,768]{2,1,0:T(2,128)(2,1)S(1)} async-done(((bf16[32,2,768]{2,1,0:T(2,128)(2,1)}), bf16[32,2,768]{2,1,0:T(2,128)(2,1)S(1)}, u32[]{:S(2)}, u32[]{:S(2)}) %all-to-all-start) | async-done | bytes 98336 | tf_op jit(solution)/shard_map/all_to_all | solution.py:60
  383.3 6.7 %reshape.187 = bf16[1024,3,4,4]{3,2,1,0:T(4,128)(2,1)S(1)} reshape(bf16[32,2,768]{2,1,0:T(2,128)(2,1)S(1)} %all-to-all-done) | data formatting | bytes 196608
  390.0 3.7 copy.58
  393.7 6.8 %reshape.180 = bf16[12,16,2,128]{3,2,1,0:T(2,128)(2,1)S(1)} reshape(bf16[4,3,32,32,4]{4,3,2,1,0:T(8,128)(2,1)} %bitcast.29) | data formatting | bytes 196608 | tf_op jit(solution)/shard_map/reshape | solution.py:77
  400.5 3.6 fusion.13
  404.1 0.5 copy.34
  404.6 0.0 copy-done
  404.6 1.9 convolution_bitcast_fusion
  406.5 1.3 copy.37
  (1 shorter events, 0.0 us)
Async XLA Ops:
  0.0 404.6 %copy-start = (f32[3,4,4]{2,1,0:T(4,128)S(1)}, f32[3,4,4]{2,1,0:T(4,128)}, u32[]{:S(2)}) copy-start(f32[3,4,4]{2,1,0:T(4,128)} %param.11) | copy-start | bytes 580
  344.2 8.4 %copy-start.1 = (bf16[3,4,4,1536]{3,2,1,0:T(4,128)(2,1)S(1)}, bf16[3,4,4,1536]{3,2,1,0:T(4,128)(2,1)}, u32[]{:S(2)}) copy-start(bf16[3,4,4,1536]{3,2,1,0:T(4,128)(2,1)} %param.6) | copy-start | bytes 442372
  368.0 15.3 %all-to-all-start = ((bf16[32,2,768]{2,1,0:T(2,128)(2,1)}), bf16[32,2,768]{2,1,0:T(2,128)(2,1)S(1)}, u32[]{:S(2)}, u32[]{:S(2)}) async-start(bf16[32,2,768]{2,1,0:T(2,128)(2,1)} %reshape.186), calls=%async_computation | async-start | bytes 196608 | tf_op jit(solution)/shard_map/all_to_all | solution.py:60
where the time goes:
time: 409 us; the launch traced here: 408 us
  other arithmetic  353 us (86%)
  local copies, waits for them, and re-layouts  29.8 us (7%)
  matrix products  10.5 us (3%)
  starting transfers between devices  7.54 us (2%)
  waiting for transfers between devices  6.93 us (2%)
    another operation x1, other arithmetic  337 us
    unnamed x6, local copies, waits for them, and re-layouts  13.6 us
    another operation x1, other arithmetic, fourier_table(): jnp.stack([jnp.cos(angles) * factor, -jnp.sin(angles) * factor], axis=-1)  8.37 us
  transfers between devices with their start and end apart: 1, of which 1 were waited for; matrix products, arithmetic and copies ran while one was open for 0% of the time, Pallas kernels for 0%

commit v1 on v0

v1 whole, which is shorter than its diff:
```python
import math

import jax
import jax.numpy as jnp
from jax import lax
from jax.experimental import pallas as pl
from jax.experimental.pallas import tpu as pltpu
from jax.sharding import PartitionSpec as P

LANES = 128
K_LOW = 32
K_TILE = 256
SIN_COEFFS = tuple(
    (-1.0) ** i * (2.0 * math.pi) ** (2 * i + 1) / math.factorial(2 * i + 1) for i in range(6)
)


def sin_quarter(v):
    s = v * v
    acc = jnp.full_like(s, SIN_COEFFS[5])
    for c in SIN_COEFFS[4::-1]:
        acc = acc * s + c
    return acc * v


def cos_sin(product, count, inverse):
    turns = jnp.floor(product * inverse + 0.5)
    u = (product - turns * count) * inverse
    cosine = sin_quarter(0.25 - jnp.abs(u))
    sine = sin_quarter(jnp.maximum(jnp.minimum(u, 0.5 - u), -0.5 - u))
    return cosine, sine


def grid_kernel(
    mix, pad, points_ref, vert_ref, grid_ref, wind_ref, order_ref, out_ref,
    x_ref, e_ref, twc_ref, tws_ref, ac_ref, as_ref,
):
    fields, levels, rows, width = grid_ref.shape
    wave_total = order_ref.shape[1]
    groups = wave_total // LANES
    pairs = fields * levels
    tiles = width // LANES

    row_id = lax.broadcasted_iota(jnp.int32, (rows, width), 0)
    positions = lax.broadcasted_iota(jnp.int32, (rows, width), 1)
    counts = jnp.zeros((rows, width), jnp.int32)
    for j in range(rows):
        counts = jnp.where(row_id == j, points_ref[j], counts)
    inside = positions < counts
    at_end = positions == counts - 1
    at_start = positions == 0
    advected = {}
    for level in range(levels):
        wind = wind_ref[level].astype(jnp.float32)
        for field in range(fields):
            g = grid_ref[field, level].astype(jnp.float32)
            flux = jnp.where(inside, wind * g, 0.0)
            first = flux[:, :1]
            last = jnp.sum(jnp.where(at_end, flux, 0.0), axis=-1, keepdims=True)
            forward = jnp.where(at_end, first, pltpu.roll(flux, width - 1, 1))
            backward = jnp.where(at_start, last, pltpu.roll(flux, 1, 1))
            result = jnp.where(inside, g + 0.5 * (forward - backward), 0.0)
            advected[field, level] = result.astype(jnp.bfloat16).astype(jnp.float32)
    for field in range(fields):
        for level in range(levels):
            if mix:
                value = vert_ref[field, 0, level] * advected[field, 0]
                for p in range(1, levels):
                    value = value + vert_ref[field, p, level] * advected[field, p]
            else:
                value = advected[field, level]
            for t in range(tiles):
                x_ref[t, pl.ds(field * levels + level, rows, stride=pad), :] = value[
                    :, t * LANES:(t + 1) * LANES
                ]
    for extra in range(pairs, pad):
        for t in range(tiles):
            x_ref[t, pl.ds(extra, rows, stride=pad), :] = jnp.zeros((rows, LANES), jnp.float32)

    shape = (rows * groups, width)
    tw_row = lax.broadcasted_iota(jnp.int32, shape, 0)
    tw_count = jnp.zeros(shape, jnp.int32)
    for j in range(rows):
        tw_count = jnp.where(tw_row // groups == j, points_ref[j], tw_count)
    tw_count = tw_count.astype(jnp.float32)
    tw_product = (
        (tw_row % groups) * LANES * lax.broadcasted_iota(jnp.int32, shape, 1)
    ).astype(jnp.float32)
    twc, tws = cos_sin(tw_product, tw_count, 1.0 / tw_count)
    twc_ref[...] = twc
    tws_ref[...] = tws

    k_high = width // K_LOW
    high = (
        K_LOW
        * lax.broadcasted_iota(jnp.int32, (k_high, LANES), 0)
        * lax.broadcasted_iota(jnp.int32, (k_high, LANES), 1)
    ).astype(jnp.float32)
    low = (
        lax.broadcasted_iota(jnp.int32, (K_LOW, LANES), 0)
        * lax.broadcasted_iota(jnp.int32, (K_LOW, LANES), 1)
    ).astype(jnp.float32)
    for j in range(rows):
        count = jnp.full((8, LANES), points_ref[j], jnp.int32).astype(jnp.float32)
        inverse = (1.0 / count)[:1]
        count = count[:1]
        ac, as_ = cos_sin(high, count, inverse)
        ac_ref[j] = ac
        as_ref[j] = as_
        bc, bs = cos_sin(low, count, inverse)
        acc = jnp.zeros(((2 * groups - 1) * pad, 2 * LANES), jnp.float32)
        for start in range(0, width, K_TILE):
            pieces = []
            for k1 in range(start // K_LOW, (start + K_TILE) // K_LOW):
                hc = ac_ref[j, pl.ds(k1, 1), :]
                hs = as_ref[j, pl.ds(k1, 1), :]
                cosine = (hc * bc - hs * bs).astype(jnp.bfloat16)
                sine = (hs * bc + hc * bs).astype(jnp.bfloat16)
                pieces.append(jnp.concatenate([cosine, sine], axis=1))
            table = jnp.concatenate(pieces, axis=0)
            x = jnp.concatenate(
                [
                    x_ref[t, pl.ds(j * pad, pad), :]
                    for t in range(start // LANES, (start + K_TILE) // LANES)
                ],
                axis=1,
            )
            left = [x.astype(jnp.bfloat16)]
            for g in range(1, groups):
                left.append(
                    (x * twc_ref[pl.ds(j * groups + g, 1), pl.ds(start, K_TILE)]).astype(jnp.bfloat16)
                )
                left.append(
                    (x * tws_ref[pl.ds(j * groups + g, 1), pl.ds(start, K_TILE)]).astype(jnp.bfloat16)
                )
            acc = acc + jnp.dot(
                jnp.concatenate(left, axis=0), table, preferred_element_type=jnp.float32
            )
        highest = (points_ref[j] - 1) // 2
        for g in range(groups):
            order = g * LANES + lax.broadcasted_iota(jnp.int32, (pad, LANES), 1)
            factor = jnp.where(order > highest, 0.0, jnp.where(order == 0, 1.0, 2.0))
            if g == 0:
                real = acc[:pad, :LANES]
                imag = acc[:pad, LANES:]
            else:
                at = (2 * g - 1) * pad
                real = acc[at:at + pad, :LANES] - acc[at + pad:at + 2 * pad, LANES:]
                imag = acc[at + pad:at + 2 * pad, :LANES] + acc[at:at + pad, LANES:]
            e_ref[g, pl.ds(j * 2 * pad, pad, stride=2), :] = real * factor
            e_ref[g, pl.ds(j * 2 * pad + 1, pad, stride=2), :] = -imag * factor

    select = (
        lax.broadcasted_iota(jnp.int32, (wave_total, wave_total), 0) == order_ref[...]
    ).astype(jnp.float32).astype(jnp.bfloat16)
    fourier = jnp.concatenate([e_ref[g].astype(jnp.bfloat16) for g in range(groups)], axis=1)
    slots = jnp.dot(fourier, select, preferred_element_type=jnp.float32)
    out_ref[...] = slots.T.astype(jnp.bfloat16)


def spectral_kernel(
    axes, sources, pad, order_ref, recv_ref, table_ref, out_ref, g_ref,
):
    step = pl.program_id(0)
    peers, fields, levels, block, _, wave_total = out_ref.shape
    lanes = recv_ref.shape[-1]
    slot_count = recv_ref.shape[1] // sources
    rows = lanes // (2 * pad)
    row_total = table_ref.shape[-1]

    @pl.when(step == 0)
    def _():
        g_ref[...] = recv_ref[...].astype(jnp.float32)

    shard = lax.axis_index(axes[0]) * lax.axis_size(axes[1]) + lax.axis_index(axes[1])
    first_slot = shard * slot_count
    spread = (
        lax.broadcasted_iota(jnp.int32, (sources, row_total), 0)
        == lax.broadcasted_iota(jnp.int32, (sources, row_total), 1) // rows
    ).astype(jnp.float32).astype(jnp.bfloat16)
    lane_row = lax.broadcasted_iota(jnp.int32, (2 * pad, row_total), 1) % rows
    degrees = lax.broadcasted_iota(jnp.int32, (2 * pad, wave_total), 1)
    for b in range(block):
        slot = step * block + b
        order = order_ref[first_slot + slot]
        for peer in range(peers):
            g = g_ref[peer, pl.ds(slot, sources, stride=slot_count), :]
            expanded = jnp.dot(
                g.T.astype(jnp.bfloat16), spread, preferred_element_type=jnp.float32
            )
            left = expanded[:2 * pad]
            for j in range(1, rows):
                left = jnp.where(lane_row == j, expanded[j * 2 * pad:(j + 1) * 2 * pad], left)
            value = lax.dot_general(
                left.astype(jnp.bfloat16), table_ref[b], (((1,), (1,)), ((), ())),
                preferred_element_type=jnp.float32,
            )
            value = jnp.where(degrees >= order, value, 0.0)
            for field in range(fields):
                for level in range(levels):
                    at = 2 * (field * levels + level)
                    out_ref[peer, field, level, b] = value[at:at + 2]


def body(grid_adjoint, courant, row_points, wave_order, legendre, vert_inverse):
    fields, levels_dev, row_count, row_width = grid_adjoint.shape
    wave_total = wave_order.shape[0]
    groups = wave_total // LANES
    sources = lax.axis_size("wave")
    peers = lax.axis_size("lev")
    pad = -(-fields * levels_dev // 16) * 16
    mix = peers == 1
    smem = pl.BlockSpec(memory_space=pltpu.SMEM)
    vmem = pl.BlockSpec(memory_space=pltpu.VMEM)
    lanes = row_count * 2 * pad
    send = pl.pallas_call(
        lambda *refs: grid_kernel(mix, pad, *refs),
        out_shape=jax.ShapeDtypeStruct((wave_total, lanes), jnp.bfloat16),
        in_specs=[smem, smem, vmem, vmem, vmem],
        out_specs=vmem,
        scratch_shapes=[
            pltpu.VMEM((row_width // LANES, row_count * pad, LANES), jnp.float32),
            pltpu.VMEM((groups, lanes, LANES), jnp.float32),
            pltpu.VMEM((row_count * groups, row_width), jnp.float32),
            pltpu.VMEM((row_count * groups, row_width), jnp.float32),
            pltpu.VMEM((row_count, row_width // K_LOW, LANES), jnp.float32),
            pltpu.VMEM((row_count, row_width // K_LOW, LANES), jnp.float32),
        ],
        name="grid_side",
    )(row_points, vert_inverse, grid_adjoint, courant, wave_order.reshape(1, wave_total))

    received = lax.all_to_all(send, "wave", split_axis=0, concat_axis=0, tiled=True)
    table = legendre
    received = received.reshape(1, sources, wave_total // sources, lanes)
    if peers > 1:
        table = lax.all_to_all(legendre, "lev", split_axis=0, concat_axis=1, tiled=True)
        received = lax.all_to_all(received, "lev", split_axis=2, concat_axis=0, tiled=True)
    slot_count, degrees, row_total = table.shape
    received = received.reshape(peers, sources * slot_count, lanes)
    block = math.gcd(4, slot_count)
    out = pl.pallas_call(
        lambda *refs: spectral_kernel(("wave", "lev"), sources, pad, *refs),
        grid=(slot_count // block,),
        out_shape=jax.ShapeDtypeStruct(
            (peers, fields, levels_dev, slot_count, 2, degrees), jnp.float32
        ),
        in_specs=[
            smem,
            vmem,
            pl.BlockSpec((block, degrees, row_total), lambda s: (s, 0, 0)),
        ],
        out_specs=pl.BlockSpec(
            (peers, fields, levels_dev, block, 2, degrees), lambda s: (0, 0, 0, s, 0, 0)
        ),
        scratch_shapes=[pltpu.VMEM((peers, sources * slot_count, lanes), jnp.float32)],
        name="spectral_side",
    )(wave_order, received, table)
    if mix:
        return out[0]
    out = jnp.transpose(out, (1, 0, 2, 3, 4, 5)).reshape(
        fields, peers * levels_dev, slot_count, 2, degrees
    )
    return jnp.einsum("fpl,fpicn->flicn", vert_inverse, out, precision=lax.Precision.HIGHEST)


def solution(mesh):
    return jax.shard_map(
        body,
        mesh=mesh,
        in_specs=(
            P(None, "lev", "wave", None),
            P("lev", "wave", None),
            P("wave"),
            P(),
            P("wave", "lev", None),
            P(),
        ),
        out_specs=P(None, None, ("wave", "lev"), None, None),
        check_vma=False,
    )
```

time: 409 us -> 25.1 us (0.06)
  other arithmetic: 353 us -> 0 us
  local copies, waits for them, and re-layouts: 29.8 us -> 0 us
  blocking collectives: 0 us -> 15.6 us
  matrix products: 10.5 us -> 0 us
  Pallas kernels: 0 us -> 9.24 us
  starting transfers between devices: 7.54 us -> 0 us
  waiting for transfers between devices: 6.93 us -> 0 us
    another operation x2 -> x0, other arithmetic: 345 us -> none
    all_to_all x0 -> x1, blocking collectives: none -> 15.6 us  [body(): lax.all_to_all(send, 'wave', split_axis=0, concat_axis=0, tiled=True)]
    unnamed x6 -> x0, local copies, waits for them, and re-layouts: 13.6 us -> none
    dot_general x3 -> x0, matrix products: 10.5 us -> none  [the longest x1 4.95 us: row_block(): lax.dot_general(advected, cosines, (((3,), (1,)), ((2,), (0,))), preferre...]
    pallas_call x0 -> x2, Pallas kernels: none -> 9.24 us  [the longest x1 5.32 us: body(): pl.pallas_call(lambda *refs: spectral_kernel(('wave', 'lev'), sources, pa...]
    all_to_all x1 -> x0, starting transfers between devices: 7.54 us -> none  [body(): lax.all_to_all(fourier, 'wave', split_axis=2, concat_axis=3, tiled=True)]
    all_to_all x1 -> x0, waiting for transfers between devices: 6.93 us -> none  [body(): lax.all_to_all(fourier, 'wave', split_axis=2, concat_axis=3, tiled=True)]
    reshape x1 -> x0, local copies, waits for them, and re-layouts: 6.77 us -> none  [body(): spectral.reshape(levels * fields, slot_count, 2, spectral.shape[-1])]
  transfers between devices with their start and end apart: 1 -> 0, of which waited for: 1 -> 0; matrix products, arithmetic and copies ran while one was open for 0% -> 0% of each run, Pallas kernels for 0% -> 0%
where the time goes in v1:
time: 25.1 us; the launch traced here: 24.9 us
  blocking collectives  15.6 us (62%)
  Pallas kernels  9.24 us (37%)
    all_to_all x1, blocking collectives, body(): lax.all_to_all(send, 'wave', split_axis=0, concat_axis=0, tiled=True)  15.6 us
    pallas_call x1, Pallas kernels, body(): pl.pallas_call(lambda *refs: spectral_kernel(('wave', 'lev'), sources, pa...  5.32 us
    pallas_call x1, Pallas kernels, body(): pl.pallas_call(lambda *refs: grid_kernel(mix, pad, *refs), out_shape=jax....  3.92 us

profile of v1, /device:TPU:0, one launch (start us, length us, event | category | flops | bytes accessed | tf_op | source)
XLA Modules:
  0.0 24.9 jit_solution(12255310544389975107)
XLA Ops:
  0.0 3.9 %grid_side.1 = bf16[512,128]{1,0:T(8,128)(2,1)} custom-call(s32[4]{0:T(128)} %refs_0_.2, f32[3,4,4]{2,1,0:T(4,128)} %refs_1_.1, bf16[3,4,4,1536]{3,2,1,0:T(4,128)(2,1)} %refs_2_.2, bf16[4,4,1536]{2,1,0:T(4,128)(2,1)} %refs_3_.1, s32[1,512]{1,0:T(1,128)} %bitcast.6), custom_call_target="tpu_custom_call" | custom-call | tf_op jit(solution)/shard_map/grid_side/pallas_call | solution.py:216
  3.9 15.6 %all_to_all.9 = bf16[32,16,128]{2,1,0:T(8,128)(2,1)} all-to-all(bf16[32,16,128]{2,1,0:T(8,128)(2,1)} %bitcast.5), channel_id=1, replica_groups=mesh['wave'=32,'lev'=1] {'wave'}, dimensions={0} | all-to-all | bytes 262144 | tf_op jit(solution)/shard_map/all_to_all | solution.py:232
  19.6 5.3 %spectral_side.1 = f32[1,3,4,16,2,512]{5,4,3,2,1,0:T(2,128)} custom-call(s32[512]{0:T(512)} %refs_0_.3, bf16[1,512,128]{2,1,0:T(8,128)(2,1)} %bitcast.4, bf16[16,512,128]{2,1,0:T(8,128)(2,1)} %refs_2_.3), custom_call_target="tpu_custom_call" | custom-call | tf_op jit(solution)/shard_map/spectral_side/pallas_call | solution.py:241

commit v2 on v1

--- a/solution.py
+++ b/solution.py
@@ -32,9 +32,15 @@
 
 
 def grid_kernel(
-    mix, pad, points_ref, vert_ref, grid_ref, wind_ref, order_ref, out_ref,
-    x_ref, e_ref, twc_ref, tws_ref, ac_ref, as_ref,
+    mix, pad, points_ref, vert_ref, grid_ref, wind_ref, order_ref, *rest
 ):
+    if mix:
+        table_hbm, out_ref, table_ref, *scratch, table_sem = rest
+        fetch = pltpu.make_async_copy(table_hbm, table_ref, table_sem)
+        fetch.start()
+    else:
+        out_ref, *scratch = rest
+    x_ref, e_ref, twc_ref, tws_ref, ac_ref, as_ref = scratch
     fields, levels, rows, width = grid_ref.shape
     wave_total = order_ref.shape[1]
     groups = wave_total // LANES
@@ -156,50 +162,72 @@
     fourier = jnp.concatenate([e_ref[g].astype(jnp.bfloat16) for g in range(groups)], axis=1)
     slots = jnp.dot(fourier, select, preferred_element_type=jnp.float32)
     out_ref[...] = slots.T.astype(jnp.bfloat16)
+    if mix:
+        fetch.wait()
 
 
 def spectral_kernel(
-    axes, sources, pad, order_ref, recv_ref, table_ref, out_ref, g_ref,
+    axes, sources, pad, groups, order_ref, recv_ref, table_ref, out_hbm, g_ref, left_ref, out_ref, sems,
 ):
-    step = pl.program_id(0)
-    peers, fields, levels, block, _, wave_total = out_ref.shape
+    peers, fields, levels, slot_count, _, wave_total = out_ref.shape
     lanes = recv_ref.shape[-1]
-    slot_count = recv_ref.shape[1] // sources
     rows = lanes // (2 * pad)
     row_total = table_ref.shape[-1]
-
-    @pl.when(step == 0)
-    def _():
-        g_ref[...] = recv_ref[...].astype(jnp.float32)
-
-    shard = lax.axis_index(axes[0]) * lax.axis_size(axes[1]) + lax.axis_index(axes[1])
-    first_slot = shard * slot_count
+    g_ref[...] = recv_ref[...].astype(jnp.float32)
+
     spread = (
         lax.broadcasted_iota(jnp.int32, (sources, row_total), 0)
         == lax.broadcasted_iota(jnp.int32, (sources, row_total), 1) // rows
     ).astype(jnp.float32).astype(jnp.bfloat16)
     lane_row = lax.broadcasted_iota(jnp.int32, (2 * pad, row_total), 1) % rows
+    for peer in range(peers):
+        blocks = [
+            g_ref[peer, pl.ds(slot, sources, stride=slot_count), :].T.astype(jnp.bfloat16)
+            for slot in range(slot_count)
+        ]
+        expanded = jnp.dot(
+            jnp.concatenate(blocks, axis=0), spread, preferred_element_type=jnp.float32
+        )
+        for slot in range(slot_count):
+            at = slot * lanes
+            left = expanded[at:at + 2 * pad]
+            for j in range(1, rows):
+                at = slot * lanes + j * 2 * pad
+                left = jnp.where(lane_row == j, expanded[at:at + 2 * pad], left)
+            left_ref[peer, slot] = left.astype(jnp.bfloat16)
+
+    shard = lax.axis_index(axes[0]) * lax.axis_size(axes[1]) + lax.axis_index(axes[1])
+    shape = (slot_count, order_ref.shape[1])
+    own = lax.broadcasted_iota(jnp.int32, shape, 1) == (
+        lax.broadcasted_iota(jnp.int32, shape, 0) + shard * slot_count
+    )
+    orders = jnp.where(own, order_ref[...].astype(jnp.float32), 0.0)
+    orders = jnp.sum(orders, axis=1, keepdims=True).astype(jnp.int32)
+
     degrees = lax.broadcasted_iota(jnp.int32, (2 * pad, wave_total), 1)
-    for b in range(block):
-        slot = step * block + b
-        order = order_ref[first_slot + slot]
+    copies = []
+    done = 0
+    for slot in range(slot_count):
+        order = orders[slot:slot + 1]
         for peer in range(peers):
-            g = g_ref[peer, pl.ds(slot, sources, stride=slot_count), :]
-            expanded = jnp.dot(
-                g.T.astype(jnp.bfloat16), spread, preferred_element_type=jnp.float32
-            )
-            left = expanded[:2 * pad]
-            for j in range(1, rows):
-                left = jnp.where(lane_row == j, expanded[j * 2 * pad:(j + 1) * 2 * pad], left)
             value = lax.dot_general(
-                left.astype(jnp.bfloat16), table_ref[b], (((1,), (1,)), ((), ())),
+                left_ref[peer, slot], table_ref[slot], (((1,), (1,)), ((), ())),
                 preferred_element_type=jnp.float32,
             )
             value = jnp.where(degrees >= order, value, 0.0)
             for field in range(fields):
                 for level in range(levels):
                     at = 2 * (field * levels + level)
-                    out_ref[peer, field, level, b] = value[at:at + 2]
+                    out_ref[peer, field, level, slot] = value[at:at + 2]
+        if slot + 1 in groups:
+            at = (slice(None), slice(None), slice(None), pl.ds(done, slot + 1 - done))
+            copies.append(
+                pltpu.make_async_copy(out_ref.at[at], out_hbm.at[at], sems.at[len(copies)])
+            )
+            copies[-1].start()
+            done = slot + 1
+    for copy in copies:
+        copy.wait()
 
 
 def body(grid_adjoint, courant, row_points, wave_order, legendre, vert_inverse):
@@ -213,48 +241,60 @@
     smem = pl.BlockSpec(memory_space=pltpu.SMEM)
     vmem = pl.BlockSpec(memory_space=pltpu.VMEM)
     lanes = row_count * 2 * pad
-    send = pl.pallas_call(
+    hbm = pl.BlockSpec(memory_space=pl.ANY)
+    out_shape = [pltpu.VMEM((wave_total, lanes), jnp.bfloat16)]
+    scratch = [
+        pltpu.VMEM((row_width // LANES, row_count * pad, LANES), jnp.float32),
+        pltpu.VMEM((groups, lanes, LANES), jnp.float32),
+        pltpu.VMEM((row_count * groups, row_width), jnp.float32),
+        pltpu.VMEM((row_count * groups, row_width), jnp.float32),
+        pltpu.VMEM((row_count, row_width // K_LOW, LANES), jnp.float32),
+        pltpu.VMEM((row_count, row_width // K_LOW, LANES), jnp.float32),
+    ]
+    operands = [row_points, vert_inverse, grid_adjoint, courant, wave_order.reshape(1, wave_total)]
+    specs = [smem, smem, vmem, vmem, vmem]
+    if mix:
+        operands.append(legendre)
+        specs.append(hbm)
+        out_shape.append(pltpu.VMEM(legendre.shape, legendre.dtype))
+        scratch.append(pltpu.SemaphoreType.DMA(()))
+    send, *table = pl.pallas_call(
         lambda *refs: grid_kernel(mix, pad, *refs),
-        out_shape=jax.ShapeDtypeStruct((wave_total, lanes), jnp.bfloat16),
-        in_specs=[smem, smem, vmem, vmem, vmem],
-        out_specs=vmem,
-        scratch_shapes=[
-            pltpu.VMEM((row_width // LANES, row_count * pad, LANES), jnp.float32),
-            pltpu.VMEM((groups, lanes, LANES), jnp.float32),
-            pltpu.VMEM((row_count * groups, row_width), jnp.float32),
-            pltpu.VMEM((row_count * groups, row_width), jnp.float32),
-            pltpu.VMEM((row_count, row_width // K_LOW, LANES), jnp.float32),
-            pltpu.VMEM((row_count, row_width // K_LOW, LANES), jnp.float32),
-        ],
+        out_shape=out_shape,
+        in_specs=specs,
+        out_specs=[vmem] * len(out_shape),
+        scratch_shapes=scratch,
         name="grid_side",
-    )(row_points, vert_inverse, grid_adjoint, courant, wave_order.reshape(1, wave_total))
+    )(*operands)
 
     received = lax.all_to_all(send, "wave", split_axis=0, concat_axis=0, tiled=True)
-    table = legendre
     received = received.reshape(1, sources, wave_total // sources, lanes)
     if peers > 1:
-        table = lax.all_to_all(legendre, "lev", split_axis=0, concat_axis=1, tiled=True)
+        table = [lax.all_to_all(legendre, "lev", split_axis=0, concat_axis=1, tiled=True)]
         received = lax.all_to_all(received, "lev", split_axis=2, concat_axis=0, tiled=True)
-    slot_count, degrees, row_total = table.shape
+    slot_count, degrees, row_total = table[0].shape
     received = received.reshape(peers, sources * slot_count, lanes)
     block = math.gcd(4, slot_count)
+    ends = tuple(range(block, slot_count + 1, block))
+    shape = (peers, fields, levels_dev, slot_count, 2, degrees)
     out = pl.pallas_call(
-        lambda *refs: spectral_kernel(("wave", "lev"), sources, pad, *refs),
-        grid=(slot_count // block,),
-        out_shape=jax.ShapeDtypeStruct(
-            (peers, fields, levels_dev, slot_count, 2, degrees), jnp.float32
-        ),
-        in_specs=[
-            smem,
-            vmem,
-            pl.BlockSpec((block, degrees, row_total), lambda s: (s, 0, 0)),
+        lambda *refs: spectral_kernel(("wave", "lev"), sources, pad, ends, *refs),
+        out_shape=jax.ShapeDtypeStruct(shape, jnp.float32),
+        in_specs=[vmem, vmem, vmem],
+        out_specs=hbm,
+        scratch_shapes=[
+            pltpu.VMEM((peers, sources * slot_count, lanes), jnp.float32),
+            pltpu.VMEM((peers, slot_count, 2 * pad, row_total), jnp.bfloat16),
+            pltpu.VMEM(shape, jnp.float32),
+            pltpu.SemaphoreType.DMA((len(ends),)),
         ],
-        out_specs=pl.BlockSpec(
-            (peers, fields, levels_dev, block, 2, degrees), lambda s: (0, 0, 0, s, 0, 0)
-        ),
-        scratch_shapes=[pltpu.VMEM((peers, sources * slot_count, lanes), jnp.float32)],
+        compiler_params=pltpu.CompilerParams(vmem_limit_bytes=16 << 20),
         name="spectral_side",
-    )(wave_order, received, table)
+    )(
+        wave_order.reshape(1, wave_total),
+        pltpu.with_memory_space_constraint(received, pltpu.VMEM),
+        pltpu.with_memory_space_constraint(table[0], pltpu.VMEM),
+    )
     if mix:
         return out[0]
     out = jnp.transpose(out, (1, 0, 2, 3, 4, 5)).reshape(

time: 25.1 us -> 20.6 us (0.82)
  Pallas kernels: 9.24 us -> 5.13 us
  blocking collectives: 15.6 us -> 15.3 us
    pallas_call x1, Pallas kernels: 5.32 us -> 1.84 us  [body(): pl.pallas_call(lambda *refs: spectral_kernel(('wave', 'lev'), sources, pa...]
    pallas_call x1, Pallas kernels: 3.92 us -> 3.29 us  [body(): pl.pallas_call(lambda *refs: grid_kernel(mix, pad, *refs), out_shape=out_...]
    all_to_all x1, blocking collectives: 15.6 us -> 15.3 us  [body(): lax.all_to_all(send, 'wave', split_axis=0, concat_axis=0, tiled=True)]
where the time goes in v2:
time: 20.6 us; the launch traced here: 20.5 us
  blocking collectives  15.3 us (74%)
  Pallas kernels  5.13 us (25%)
    all_to_all x1, blocking collectives, body(): lax.all_to_all(send, 'wave', split_axis=0, concat_axis=0, tiled=True)  15.3 us
    pallas_call x1, Pallas kernels, body(): pl.pallas_call(lambda *refs: grid_kernel(mix, pad, *refs), out_shape=out_...  3.29 us
    pallas_call x1, Pallas kernels, body(): pl.pallas_call(lambda *refs: spectral_kernel(('wave', 'lev'), sources, pa...  1.84 us

profile of v2, /device:TPU:0, one launch (start us, length us, event | category | flops | bytes accessed | tf_op | source)
XLA Modules:
  0.0 20.5 jit_solution(4160840411961658368)
XLA Ops:
  0.0 0.0 copy-start
  0.0 3.3 %grid_side.1 = (bf16[512,128]{1,0:T(8,128)(2,1)S(1)}, bf16[16,512,128]{2,1,0:T(8,128)(2,1)S(1)}) custom-call(s32[4]{0:T(128)} %refs_0_.1, f32[3,4,4]{2,1,0:T(4,128)} %refs_1_.1, bf16[3,4,4,1536]{3,2,1,0:T(4,128)(2,1)} %refs_2_.1, bf16[4,4,1536]{2,1,0:T(4,128)(2,1)} %refs_3_.1, s32[1,512]{1,0:T(1,128)} %bitcast.6, bf16[16,512,128]{2,1,0:T(8,128)(2,1)} %refs_5_.1), custom_call_target="tpu_custom_call" | custom-call | tf_op jit(solution)/shard_map/grid_side/pallas_call | solution.py:261
  3.3 15.3 %all_to_all.9 = bf16[32,16,128]{2,1,0:T(8,128)(2,1)S(1)} all-to-all(bf16[32,16,128]{2,1,0:T(8,128)(2,1)S(1)} %bitcast.5), channel_id=1, replica_groups=mesh['wave'=32,'lev'=1] {'wave'}, dimensions={0} | all-to-all | bytes 262144 | tf_op jit(solution)/shard_map/all_to_all | solution.py:270
  18.6 0.0 copy-done
  18.6 1.8 %spectral_side.1 = f32[1,3,4,16,2,512]{5,4,3,2,1,0:T(2,128)} custom-call(s32[1,512]{1,0:T(1,128)S(1)} %bitcast.7, bf16[1,512,128]{2,1,0:T(8,128)(2,1)S(1)} %bitcast.4, bf16[16,512,128]{2,1,0:T(8,128)(2,1)S(1)} %get-tuple-element.8.refs_2_), custom_call_target="tpu_custom_call" | custom-call | tf_op jit(solution)/shard_map/spectral_side/pallas_call | solution.py:280
Async XLA Ops:
  0.0 18.6 %copy-start = (s32[512]{0:T(512)S(1)}, s32[512]{0:T(512)}, u32[]{:S(2)}) copy-start(s32[512]{0:T(512)} %param.9) | copy-start | bytes 6148

commit v3 on v2

--- a/solution.py
+++ b/solution.py
@@ -8,8 +8,7 @@
 from jax.sharding import PartitionSpec as P
 
 LANES = 128
-K_LOW = 32
-K_TILE = 256
+HALF = 16
 SIN_COEFFS = tuple(
     (-1.0) ** i * (2.0 * math.pi) ** (2 * i + 1) / math.factorial(2 * i + 1) for i in range(6)
 )
@@ -17,8 +16,8 @@
 
 def sin_quarter(v):
     s = v * v
-    acc = jnp.full_like(s, SIN_COEFFS[5])
-    for c in SIN_COEFFS[4::-1]:
+    acc = SIN_COEFFS[5] * s + SIN_COEFFS[4]
+    for c in SIN_COEFFS[3::-1]:
         acc = acc * s + c
     return acc * v
 
@@ -31,133 +30,233 @@
     return cosine, sine
 
 
+def iota(shape, axis):
+    return lax.broadcasted_iota(jnp.int32, shape, axis)
+
+
+def within_tile(lane):
+    inner = lane % (2 * HALF)
+    return lane - inner + jnp.where(inner < HALF, HALF + inner, 2 * HALF - 1 - inner)
+
+
 def grid_kernel(
-    mix, pad, points_ref, vert_ref, grid_ref, wind_ref, order_ref, *rest
+    mix, pad, points_hbm, vert_hbm, grid_hbm, wind_hbm, order_hbm, *rest
 ):
     if mix:
         table_hbm, out_ref, table_ref, *scratch, table_sem = rest
         fetch = pltpu.make_async_copy(table_hbm, table_ref, table_sem)
-        fetch.start()
     else:
         out_ref, *scratch = rest
-    x_ref, e_ref, twc_ref, tws_ref, ac_ref, as_ref = scratch
-    fields, levels, rows, width = grid_ref.shape
+    (
+        grid_buf, wind_buf, g_ref, f_ref, x_ref, t_ref, e_ref,
+        twc_ref, tws_ref, ac_ref, as_ref, turn_ref, mix_ref,
+        points_ref, vert_ref, order_ref, points_sem, vert_sem, order_sem, grid_sem, wind_sem,
+    ) = scratch
+    points_copy = pltpu.make_async_copy(points_hbm, points_ref, points_sem)
+    points_copy.start()
+    vert_copy = pltpu.make_async_copy(vert_hbm, vert_ref, vert_sem)
+    order_copy = pltpu.make_async_copy(order_hbm, order_ref, order_sem)
+    grid_copy = pltpu.make_async_copy(grid_hbm, grid_buf, grid_sem)
+    wind_copy = pltpu.make_async_copy(wind_hbm, wind_buf, wind_sem)
+    grid_copy.start()
+    wind_copy.start()
+    vert_copy.start()
+    order_copy.start()
+    if mix:
+        fetch.start()
+    fields, levels, rows, width = grid_buf.shape
     wave_total = order_ref.shape[1]
     groups = wave_total // LANES
     pairs = fields * levels
     tiles = width // LANES
-
-    row_id = lax.broadcasted_iota(jnp.int32, (rows, width), 0)
-    positions = lax.broadcasted_iota(jnp.int32, (rows, width), 1)
-    counts = jnp.zeros((rows, width), jnp.int32)
-    for j in range(rows):
-        counts = jnp.where(row_id == j, points_ref[j], counts)
-    inside = positions < counts
-    at_end = positions == counts - 1
-    at_start = positions == 0
-    advected = {}
-    for level in range(levels):
-        wind = wind_ref[level].astype(jnp.float32)
-        for field in range(fields):
-            g = grid_ref[field, level].astype(jnp.float32)
-            flux = jnp.where(inside, wind * g, 0.0)
-            first = flux[:, :1]
-            last = jnp.sum(jnp.where(at_end, flux, 0.0), axis=-1, keepdims=True)
-            forward = jnp.where(at_end, first, pltpu.roll(flux, width - 1, 1))
-            backward = jnp.where(at_start, last, pltpu.roll(flux, 1, 1))
-            result = jnp.where(inside, g + 0.5 * (forward - backward), 0.0)
-            advected[field, level] = result.astype(jnp.bfloat16).astype(jnp.float32)
-    for field in range(fields):
-        for level in range(levels):
-            if mix:
-                value = vert_ref[field, 0, level] * advected[field, 0]
-                for p in range(1, levels):
-                    value = value + vert_ref[field, p, level] * advected[field, p]
-            else:
-                value = advected[field, level]
-            for t in range(tiles):
-                x_ref[t, pl.ds(field * levels + level, rows, stride=pad), :] = value[
-                    :, t * LANES:(t + 1) * LANES
-                ]
-    for extra in range(pairs, pad):
-        for t in range(tiles):
-            x_ref[t, pl.ds(extra, rows, stride=pad), :] = jnp.zeros((rows, LANES), jnp.float32)
-
-    shape = (rows * groups, width)
-    tw_row = lax.broadcasted_iota(jnp.int32, shape, 0)
-    tw_count = jnp.zeros(shape, jnp.int32)
-    for j in range(rows):
-        tw_count = jnp.where(tw_row // groups == j, points_ref[j], tw_count)
-    tw_count = tw_count.astype(jnp.float32)
-    tw_product = (
-        (tw_row % groups) * LANES * lax.broadcasted_iota(jnp.int32, shape, 1)
-    ).astype(jnp.float32)
-    twc, tws = cos_sin(tw_product, tw_count, 1.0 / tw_count)
+    half_tiles = -(-width // (2 * LANES))
+    half_width = half_tiles * LANES
+
+    points_copy.wait()
+
+    shape = (rows * groups, half_width)
+    row_id = iota(shape, 0)
+    count = jnp.zeros(shape, jnp.int32)
+    for j in range(rows):
+        count = jnp.where(row_id // groups == j, 2 * points_ref[j], count)
+    count = count.astype(jnp.float32)
+    lane = iota(shape, 1)
+    product = ((row_id % groups) * LANES * (2 * within_tile(lane) + 1)).astype(jnp.float32)
+    twc, tws = cos_sin(product, count, 1.0 / count)
     twc_ref[...] = twc
     tws_ref[...] = tws
 
-    k_high = width // K_LOW
-    high = (
-        K_LOW
-        * lax.broadcasted_iota(jnp.int32, (k_high, LANES), 0)
-        * lax.broadcasted_iota(jnp.int32, (k_high, LANES), 1)
-    ).astype(jnp.float32)
-    low = (
-        lax.broadcasted_iota(jnp.int32, (K_LOW, LANES), 0)
-        * lax.broadcasted_iota(jnp.int32, (K_LOW, LANES), 1)
-    ).astype(jnp.float32)
-    for j in range(rows):
-        count = jnp.full((8, LANES), points_ref[j], jnp.int32).astype(jnp.float32)
+    shape = (max(rows, 8), wave_total)
+    row_id = iota(shape, 0)
+    count = jnp.full(shape, 2 * points_ref[0], jnp.int32)
+    for j in range(1, rows):
+        count = jnp.where(row_id == j, 2 * points_ref[j], count)
+    wave = iota(shape, 1)
+    weight = jnp.where(2 * wave > count // 2 - 1, 0.0, jnp.where(wave == 0, 1.0, 2.0))
+    count = count.astype(jnp.float32)
+    cosine, sine = cos_sin(wave.astype(jnp.float32), count, 1.0 / count)
+    turn_ref[0] = cosine * weight
+    turn_ref[1] = sine * weight
+
+    blocks = half_width // (2 * HALF)
+    high = (iota((blocks, LANES), 1) * (4 * HALF * iota((blocks, LANES), 0) + 2 * HALF)).astype(
+        jnp.float32
+    )
+    low = (iota((HALF, LANES), 1) * (2 * iota((HALF, LANES), 0) + 1)).astype(jnp.float32)
+    for j in range(rows):
+        count = jnp.full((8, LANES), 2 * points_ref[j], jnp.int32).astype(jnp.float32)
         inverse = (1.0 / count)[:1]
         count = count[:1]
         ac, as_ = cos_sin(high, count, inverse)
         ac_ref[j] = ac
         as_ref[j] = as_
         bc, bs = cos_sin(low, count, inverse)
-        acc = jnp.zeros(((2 * groups - 1) * pad, 2 * LANES), jnp.float32)
-        for start in range(0, width, K_TILE):
-            pieces = []
-            for k1 in range(start // K_LOW, (start + K_TILE) // K_LOW):
-                hc = ac_ref[j, pl.ds(k1, 1), :]
-                hs = as_ref[j, pl.ds(k1, 1), :]
-                cosine = (hc * bc - hs * bs).astype(jnp.bfloat16)
-                sine = (hs * bc + hc * bs).astype(jnp.bfloat16)
-                pieces.append(jnp.concatenate([cosine, sine], axis=1))
-            table = jnp.concatenate(pieces, axis=0)
-            x = jnp.concatenate(
-                [
-                    x_ref[t, pl.ds(j * pad, pad), :]
-                    for t in range(start // LANES, (start + K_TILE) // LANES)
-                ],
-                axis=1,
+        for block in range(blocks):
+            hc = ac_ref[j, pl.ds(block, 1), :]
+            hs = as_ref[j, pl.ds(block, 1), :]
+            cc, ss, sc, cs = hc * bc, hs * bs, hs * bc, hc * bs
+            at = 2 * HALF * block
+            t_ref[j, pl.ds(at, HALF), :] = (cc - ss).astype(jnp.bfloat16)
+            t_ref[j, pl.ds(at + HALF, HALF), :] = (cc + ss).astype(jnp.bfloat16)
+            at += half_width
+            t_ref[j, pl.ds(at, HALF), :] = (sc + cs).astype(jnp.bfloat16)
+            t_ref[j, pl.ds(at + HALF, HALF), :] = (sc - cs).astype(jnp.bfloat16)
+
+    vert_copy.wait()
+    if mix:
+        mix_ref[...] = jnp.zeros_like(mix_ref)
+        lane = iota((1, LANES), 1)
+        for field in range(fields):
+            for level in range(levels):
+                row = jnp.zeros((1, LANES), jnp.float32)
+                for p in range(levels):
+                    hit = (lane % pad == field * levels + p) & (lane < 3 * pad)
+                    row = jnp.where(hit, vert_ref[field, p, level], row)
+                mix_ref[pl.ds(field * levels + level, 1), :] = row
+        full = mix_ref[...]
+        first = full.astype(jnp.bfloat16).astype(jnp.float32)
+        second = (full - first).astype(jnp.bfloat16).astype(jnp.float32)
+        third = full - first - second
+        lane = iota((pad, LANES), 1)
+        matrix = jnp.where(lane < pad, first, jnp.where(lane < 2 * pad, second, third))
+        matrix = matrix[:, :3 * pad].astype(jnp.bfloat16)
+
+    order_copy.wait()
+    wind_copy.wait()
+    grid_copy.wait()
+    half_pad = pad // 2
+    shape = (rows * pad, pairs * rows)
+    pick = (iota(shape, 0) % pad * rows + iota(shape, 0) // pad == iota(shape, 1)) & (
+        iota(shape, 0) % pad < pairs
+    )
+    grid_rows = jnp.dot(
+        pick.astype(jnp.float32).astype(jnp.bfloat16),
+        grid_buf[...].reshape(pairs * rows, width),
+        preferred_element_type=jnp.float32,
+    )
+    shape = (rows * half_pad, levels * rows)
+    pick = iota(shape, 0) % levels * rows + iota(shape, 0) // half_pad == iota(shape, 1)
+    wind_rows = jnp.dot(
+        jnp.where(pick, 0.5, 0.0).astype(jnp.bfloat16),
+        wind_buf[...].reshape(levels * rows, width),
+        preferred_element_type=jnp.float32,
+    )
+    for j in range(rows):
+        for t in range(tiles):
+            at = slice(t * LANES, (t + 1) * LANES)
+            g = grid_rows[j * pad:(j + 1) * pad, at]
+            w = wind_rows[j * half_pad:(j + 1) * half_pad, at]
+            g_ref[j, t] = g
+            f_ref[j, t + 1] = g * jnp.concatenate([w, w], axis=0)
+
+    lane = iota((pad, LANES), 1)
+    point = within_tile(lane)
+    for j in range(rows):
+        length = points_ref[j]
+        next_tile = length // LANES
+        next_lane = length % LANES
+        f_ref[j, 0] = pltpu.roll(
+            f_ref[j, (length - 1) // LANES + 1], LANES - 1 - (length - 1) % LANES, 1
+        )
+        f_ref[j, tiles + 1] = jnp.zeros((pad, LANES), jnp.float32)
+        f_ref[j, next_tile + 1] = jnp.where(
+            lane == next_lane, pltpu.roll(f_ref[j, 1], next_lane, 1), f_ref[j, next_tile + 1]
+        )
+    advected = []
+    for j in range(rows):
+        flux = [f_ref[j, t] for t in range(tiles + 2)]
+        ahead = [pltpu.roll(f, LANES - 1, 1) for f in flux[1:]]
+        behind = [pltpu.roll(f, 1, 1) for f in flux[:-1]]
+        parts = []
+        for t in range(tiles):
+            forward = jnp.where(lane == LANES - 1, ahead[t + 1], ahead[t])
+            backward = jnp.where(lane == 0, behind[t], behind[t + 1])
+            parts.append((g_ref[j, t] + (forward - backward)).astype(jnp.bfloat16))
+        advected.append(jnp.concatenate(parts, axis=1))
+    for j in range(rows):
+        if mix:
+            mixed = jnp.dot(
+                matrix, jnp.concatenate([advected[j]] * 3, axis=0),
+                preferred_element_type=jnp.float32,
             )
-            left = [x.astype(jnp.bfloat16)]
-            for g in range(1, groups):
-                left.append(
-                    (x * twc_ref[pl.ds(j * groups + g, 1), pl.ds(start, K_TILE)]).astype(jnp.bfloat16)
+        else:
+            mixed = advected[j].astype(jnp.float32)
+        for t in range(tiles):
+            x_ref[j, half_tiles + t] = mixed[:, t * LANES:(t + 1) * LANES]
+
+    products = []
+    for j in range(rows):
+        length = points_ref[j]
+        last_tile = (length - 1) // LANES
+        last_lane = (length - 1) % LANES
+        mirror = (last_lane - point) & (LANES - 1)
+        mirrored = [
+            jnp.take_along_axis(x_ref[j, half_tiles + last_tile - t], mirror, axis=1)
+            for t in range(half_tiles + 1)
+        ]
+        even = []
+        odd = []
+        for t in range(half_tiles):
+            value = jnp.take_along_axis(x_ref[j, half_tiles + t], point, axis=1)
+            other = jnp.where(point <= last_lane, mirrored[t], mirrored[t + 1])
+            paired = 2 * (point + t * LANES) < length - 1
+            kept = 2 * (point + t * LANES) <= length - 1
+            other = jnp.where(paired, other, 0.0)
+            even.append(jnp.where(kept, value, 0.0) + other)
+            odd.append(jnp.where(paired, value, 0.0) - other)
+        even = jnp.concatenate(even, axis=1)
+        odd = jnp.concatenate(odd, axis=1)
+
+        real = [jnp.concatenate([even.astype(jnp.bfloat16), jnp.zeros(even.shape, jnp.bfloat16)], 1)]
+        imag = [jnp.concatenate([jnp.zeros(odd.shape, jnp.bfloat16), odd.astype(jnp.bfloat16)], 1)]
+        for g in range(1, groups):
+            c = twc_ref[pl.ds(j * groups + g, 1), :]
+            s = tws_ref[pl.ds(j * groups + g, 1), :]
+            real.append(
+                jnp.concatenate(
+                    [(even * c).astype(jnp.bfloat16), (even * -s).astype(jnp.bfloat16)], axis=1
                 )
-                left.append(
-                    (x * tws_ref[pl.ds(j * groups + g, 1), pl.ds(start, K_TILE)]).astype(jnp.bfloat16)
+            )
+            imag.append(
+                jnp.concatenate(
+                    [(odd * s).astype(jnp.bfloat16), (odd * c).astype(jnp.bfloat16)], axis=1
                 )
-            acc = acc + jnp.dot(
-                jnp.concatenate(left, axis=0), table, preferred_element_type=jnp.float32
             )
-        highest = (points_ref[j] - 1) // 2
+        left = jnp.concatenate(real + imag, axis=0)
+
+        products.append(jnp.dot(left, t_ref[j], preferred_element_type=jnp.float32))
+    for j in range(rows):
+        product = products[j]
         for g in range(groups):
-            order = g * LANES + lax.broadcasted_iota(jnp.int32, (pad, LANES), 1)
-            factor = jnp.where(order > highest, 0.0, jnp.where(order == 0, 1.0, 2.0))
-            if g == 0:
-                real = acc[:pad, :LANES]
-                imag = acc[:pad, LANES:]
-            else:
-                at = (2 * g - 1) * pad
-                real = acc[at:at + pad, :LANES] - acc[at + pad:at + 2 * pad, LANES:]
-                imag = acc[at + pad:at + 2 * pad, :LANES] + acc[at:at + pad, LANES:]
-            e_ref[g, pl.ds(j * 2 * pad, pad, stride=2), :] = real * factor
-            e_ref[g, pl.ds(j * 2 * pad + 1, pad, stride=2), :] = -imag * factor
+            yr = product[g * pad:(g + 1) * pad]
+            yi = product[(groups + g) * pad:(groups + g + 1) * pad]
+            c = turn_ref[0, pl.ds(j, 1), pl.ds(g * LANES, LANES)]
+            s = turn_ref[1, pl.ds(j, 1), pl.ds(g * LANES, LANES)]
+            e_ref[g, pl.ds(j * 2 * pad, pad, stride=2), :] = c * yr + s * yi
+            e_ref[g, pl.ds(j * 2 * pad + 1, pad, stride=2), :] = s * yr - c * yi
 
     select = (
-        lax.broadcasted_iota(jnp.int32, (wave_total, wave_total), 0) == order_ref[...]
+        iota((wave_total, wave_total), 0) == order_ref[...]
     ).astype(jnp.float32).astype(jnp.bfloat16)
     fourier = jnp.concatenate([e_ref[g].astype(jnp.bfloat16) for g in range(groups)], axis=1)
     slots = jnp.dot(fourier, select, preferred_element_type=jnp.float32)
@@ -243,16 +342,31 @@
     lanes = row_count * 2 * pad
     hbm = pl.BlockSpec(memory_space=pl.ANY)
     out_shape = [pltpu.VMEM((wave_total, lanes), jnp.bfloat16)]
+    tiles = row_width // LANES
+    half_tiles = -(-row_width // (2 * LANES))
+    half_width = half_tiles * LANES
+    blocks = half_width // (2 * HALF)
     scratch = [
-        pltpu.VMEM((row_width // LANES, row_count * pad, LANES), jnp.float32),
+        pltpu.VMEM(grid_adjoint.shape, grid_adjoint.dtype),
+        pltpu.VMEM(courant.shape, courant.dtype),
+        pltpu.VMEM((row_count, tiles, pad, LANES), jnp.float32),
+        pltpu.VMEM((row_count, tiles + 2, pad, LANES), jnp.float32),
+        pltpu.VMEM((row_count, half_tiles + tiles, pad, LANES), jnp.float32),
+        pltpu.VMEM((row_count, 2 * half_width, LANES), jnp.bfloat16),
         pltpu.VMEM((groups, lanes, LANES), jnp.float32),
-        pltpu.VMEM((row_count * groups, row_width), jnp.float32),
-        pltpu.VMEM((row_count * groups, row_width), jnp.float32),
-        pltpu.VMEM((row_count, row_width // K_LOW, LANES), jnp.float32),
-        pltpu.VMEM((row_count, row_width // K_LOW, LANES), jnp.float32),
+        pltpu.VMEM((row_count * groups, half_width), jnp.float32),
+        pltpu.VMEM((row_count * groups, half_width), jnp.float32),
+        pltpu.VMEM((row_count, blocks, LANES), jnp.float32),
+        pltpu.VMEM((row_count, blocks, LANES), jnp.float32),
+        pltpu.VMEM((2, max(row_count, 8), wave_total), jnp.float32),
+        pltpu.VMEM((pad, LANES), jnp.float32),
+        pltpu.SMEM(row_points.shape, row_points.dtype),
+        pltpu.SMEM(vert_inverse.shape, vert_inverse.dtype),
+        pltpu.VMEM((1, wave_total), jnp.int32),
+        *[pltpu.SemaphoreType.DMA(())] * 5,
     ]
     operands = [row_points, vert_inverse, grid_adjoint, courant, wave_order.reshape(1, wave_total)]
-    specs = [smem, smem, vmem, vmem, vmem]
+    specs = [hbm] * 5
     if mix:
         operands.append(legendre)
         specs.append(hbm)

time: 20.6 us -> 20.6 us (level)
  no operation moved by 1% of the time
where the time goes in v3:
time: 20.6 us; the launch traced here: 20.4 us
  blocking collectives  15.3 us (74%)
  Pallas kernels  5.05 us (25%)
    all_to_all x1, blocking collectives, body(): lax.all_to_all(send, 'wave', split_axis=0, concat_axis=0, tiled=True)  15.3 us
    pallas_call x1, Pallas kernels, body(): pl.pallas_call(lambda *refs: grid_kernel(mix, pad, *refs), out_shape=out_...  3.22 us
    pallas_call x1, Pallas kernels, body(): pl.pallas_call(lambda *refs: spectral_kernel(('wave', 'lev'), sources, pa...  1.84 us

profile of v3, /device:TPU:0, one launch (start us, length us, event | category | flops | bytes accessed | tf_op | source)
XLA Modules:
  0.0 20.4 jit_solution(15688311038734942677)
XLA Ops:
  0.0 0.0 copy-start
  0.0 3.2 %grid_side.1 = (bf16[512,128]{1,0:T(8,128)(2,1)S(1)}, bf16[16,512,128]{2,1,0:T(8,128)(2,1)S(1)}) custom-call(s32[4]{0:T(128)} %refs_0_.1, f32[3,4,4]{2,1,0:T(4,128)} %refs_1_.1, bf16[3,4,4,1536]{3,2,1,0:T(4,128)(2,1)} %refs_2_.1, bf16[4,4,1536]{2,1,0:T(4,128)(2,1)} %refs_3_.1, s32[1,512]{1,0:T(1,128)} %bitcast.6, bf16[16,512,128]{2,1,0:T(8,128)(2,1)} %refs_5_.1), custom_call_target="tpu_custom_call" | custom-call | tf_op jit(solution)/shard_map/grid_side/pallas_call | solution.py:375
  3.2 15.3 %all_to_all.9 = bf16[32,16,128]{2,1,0:T(8,128)(2,1)S(1)} all-to-all(bf16[32,16,128]{2,1,0:T(8,128)(2,1)S(1)} %bitcast.5), channel_id=1, replica_groups=mesh['wave'=32,'lev'=1] {'wave'}, dimensions={0} | all-to-all | bytes 262144 | tf_op jit(solution)/shard_map/all_to_all | solution.py:384
  18.6 0.0 copy-done
  18.6 1.8 %spectral_side.1 = f32[1,3,4,16,2,512]{5,4,3,2,1,0:T(2,128)} custom-call(s32[1,512]{1,0:T(1,128)S(1)} %bitcast.7, bf16[1,512,128]{2,1,0:T(8,128)(2,1)S(1)} %bitcast.4, bf16[16,512,128]{2,1,0:T(8,128)(2,1)S(1)} %get-tuple-element.8.refs_2_), custom_call_target="tpu_custom_call" | custom-call | tf_op jit(solution)/shard_map/spectral_side/pallas_call | solution.py:394
Async XLA Ops:
  0.0 18.6 %copy-start = (s32[512]{0:T(512)S(1)}, s32[512]{0:T(512)}, u32[]{:S(2)}) copy-start(s32[512]{0:T(512)} %param.9) | copy-start | bytes 6148

commit v4 on v3

--- a/solution.py
+++ b/solution.py
@@ -252,47 +252,82 @@
             yi = product[(groups + g) * pad:(groups + g + 1) * pad]
             c = turn_ref[0, pl.ds(j, 1), pl.ds(g * LANES, LANES)]
             s = turn_ref[1, pl.ds(j, 1), pl.ds(g * LANES, LANES)]
-            e_ref[g, pl.ds(j * 2 * pad, pad, stride=2), :] = c * yr + s * yi
-            e_ref[g, pl.ds(j * 2 * pad + 1, pad, stride=2), :] = s * yr - c * yi
+            e_ref[g, pl.ds(j * 2 * pairs, pairs, stride=2), :] = (c * yr + s * yi)[:pairs]
+            e_ref[g, pl.ds(j * 2 * pairs + 1, pairs, stride=2), :] = (s * yr - c * yi)[:pairs]
 
     select = (
         iota((wave_total, wave_total), 0) == order_ref[...]
     ).astype(jnp.float32).astype(jnp.bfloat16)
     fourier = jnp.concatenate([e_ref[g].astype(jnp.bfloat16) for g in range(groups)], axis=1)
     slots = jnp.dot(fourier, select, preferred_element_type=jnp.float32)
-    out_ref[...] = slots.T.astype(jnp.bfloat16)
+    used = rows * 2 * pairs
+    spare = LANES - used
+    if mix:
+        chunks = used // spare
+        moved = out_ref.shape[2]
+        slot_count = moved * (chunks + 1)
+        slot = iota((spare, wave_total), 1) % slot_count
+        extra = jnp.zeros((spare, wave_total), jnp.float32)
+        for q in range(chunks):
+            shift = LANES - (chunks - q) * moved
+            part = jnp.concatenate(
+                [
+                    pltpu.roll(
+                        slots[q * spare:(q + 1) * spare, g * LANES:(g + 1) * LANES], shift, 1
+                    )
+                    for g in range(groups)
+                ],
+                axis=1,
+            )
+            extra = jnp.where(slot // moved == q, part, extra)
+        payload = jnp.concatenate([slots, extra], axis=0).T
+        payload = payload.reshape(wave_total // slot_count, chunks + 1, moved, LANES)
+        out_ref[...] = payload[:, :chunks].astype(jnp.bfloat16)
+    else:
+        blank = jnp.zeros((spare, wave_total), jnp.float32)
+        out_ref[...] = jnp.concatenate([slots, blank], axis=0).T.astype(jnp.bfloat16)
     if mix:
         fetch.wait()
 
 
 def spectral_kernel(
-    axes, sources, pad, groups, order_ref, recv_ref, table_ref, out_hbm, g_ref, left_ref, out_ref, sems,
+    axes, sources, packed, groups, order_ref, recv_ref, table_ref, out_hbm,
+    g_ref, left_ref, out_ref, sems,
 ):
     peers, fields, levels, slot_count, _, wave_total = out_ref.shape
-    lanes = recv_ref.shape[-1]
-    rows = lanes // (2 * pad)
     row_total = table_ref.shape[-1]
-    g_ref[...] = recv_ref[...].astype(jnp.float32)
+    rows = row_total // sources
+    height = 2 * fields * levels
+    used = rows * height
+    spare = LANES - used
+    g_ref[...] = recv_ref[...].astype(jnp.float32).reshape(g_ref.shape)
 
     spread = (
-        lax.broadcasted_iota(jnp.int32, (sources, row_total), 0)
-        == lax.broadcasted_iota(jnp.int32, (sources, row_total), 1) // rows
+        iota((sources, row_total), 0) == iota((sources, row_total), 1) // rows
     ).astype(jnp.float32).astype(jnp.bfloat16)
-    lane_row = lax.broadcasted_iota(jnp.int32, (2 * pad, row_total), 1) % rows
+    lane_row = iota((height, row_total), 1) % rows
+    sent = g_ref.shape[1] // sources
     for peer in range(peers):
-        blocks = [
-            g_ref[peer, pl.ds(slot, sources, stride=slot_count), :].T.astype(jnp.bfloat16)
-            for slot in range(slot_count)
+        turned = [
+            g_ref[peer, pl.ds(slot, sources, stride=sent), :].T.astype(jnp.bfloat16)
+            for slot in range(sent)
         ]
+        blocks = [value[:used] for value in turned]
+        if packed:
+            moved = slot_count - sent
+            for t in range(moved):
+                blocks.append(
+                    jnp.concatenate([value[used:] for value in turned[t::moved]], axis=0)
+                )
         expanded = jnp.dot(
             jnp.concatenate(blocks, axis=0), spread, preferred_element_type=jnp.float32
         )
         for slot in range(slot_count):
-            at = slot * lanes
-            left = expanded[at:at + 2 * pad]
+            at = slot * used
+            left = expanded[at:at + height]
             for j in range(1, rows):
-                at = slot * lanes + j * 2 * pad
-                left = jnp.where(lane_row == j, expanded[at:at + 2 * pad], left)
+                at = slot * used + j * height
+                left = jnp.where(lane_row == j, expanded[at:at + height], left)
             left_ref[peer, slot] = left.astype(jnp.bfloat16)
 
     shard = lax.axis_index(axes[0]) * lax.axis_size(axes[1]) + lax.axis_index(axes[1])
@@ -303,7 +338,7 @@
     orders = jnp.where(own, order_ref[...].astype(jnp.float32), 0.0)
     orders = jnp.sum(orders, axis=1, keepdims=True).astype(jnp.int32)
 
-    degrees = lax.broadcasted_iota(jnp.int32, (2 * pad, wave_total), 1)
+    degrees = iota((height, wave_total), 1)
     copies = []
     done = 0
     for slot in range(slot_count):
@@ -339,9 +374,13 @@
     mix = peers == 1
     smem = pl.BlockSpec(memory_space=pltpu.SMEM)
     vmem = pl.BlockSpec(memory_space=pltpu.VMEM)
-    lanes = row_count * 2 * pad
+    slot_count = wave_total // sources
+    used = row_count * 2 * fields * levels_dev
+    chunks = used // (LANES - used)
+    moved = slot_count // (chunks + 1)
+    packet = (sources, chunks, moved, LANES) if mix else (wave_total, LANES)
     hbm = pl.BlockSpec(memory_space=pl.ANY)
-    out_shape = [pltpu.VMEM((wave_total, lanes), jnp.bfloat16)]
+    out_shape = [pltpu.VMEM(packet, jnp.bfloat16)]
     tiles = row_width // LANES
     half_tiles = -(-row_width // (2 * LANES))
     half_width = half_tiles * LANES
@@ -353,7 +392,7 @@
         pltpu.VMEM((row_count, tiles + 2, pad, LANES), jnp.float32),
         pltpu.VMEM((row_count, half_tiles + tiles, pad, LANES), jnp.float32),
         pltpu.VMEM((row_count, 2 * half_width, LANES), jnp.bfloat16),
-        pltpu.VMEM((groups, lanes, LANES), jnp.float32),
+        pltpu.VMEM((groups, used, LANES), jnp.float32),
         pltpu.VMEM((row_count * groups, half_width), jnp.float32),
         pltpu.VMEM((row_count * groups, half_width), jnp.float32),
         pltpu.VMEM((row_count, blocks, LANES), jnp.float32),
@@ -382,23 +421,26 @@
     )(*operands)
 
     received = lax.all_to_all(send, "wave", split_axis=0, concat_axis=0, tiled=True)
-    received = received.reshape(1, sources, wave_total // sources, lanes)
+    sent = chunks * moved
     if peers > 1:
+        received = received.reshape(1, sources, slot_count, LANES)
         table = [lax.all_to_all(legendre, "lev", split_axis=0, concat_axis=1, tiled=True)]
         received = lax.all_to_all(received, "lev", split_axis=2, concat_axis=0, tiled=True)
     slot_count, degrees, row_total = table[0].shape
-    received = received.reshape(peers, sources * slot_count, lanes)
+    if peers > 1:
+        sent = slot_count
+        received = received.reshape(peers, sources * sent, LANES)
     block = math.gcd(4, slot_count)
     ends = tuple(range(block, slot_count + 1, block))
     shape = (peers, fields, levels_dev, slot_count, 2, degrees)
     out = pl.pallas_call(
-        lambda *refs: spectral_kernel(("wave", "lev"), sources, pad, ends, *refs),
+        lambda *refs: spectral_kernel(("wave", "lev"), sources, mix, ends, *refs),
         out_shape=jax.ShapeDtypeStruct(shape, jnp.float32),
         in_specs=[vmem, vmem, vmem],
         out_specs=hbm,
         scratch_shapes=[
-            pltpu.VMEM((peers, sources * slot_count, lanes), jnp.float32),
-            pltpu.VMEM((peers, slot_count, 2 * pad, row_total), jnp.bfloat16),
+            pltpu.VMEM((peers, sources * sent, LANES), jnp.float32),
+            pltpu.VMEM((peers, slot_count, 2 * fields * levels_dev, row_total), jnp.bfloat16),
             pltpu.VMEM(shape, jnp.float32),
             pltpu.SemaphoreType.DMA((len(ends),)),
         ],

time: 20.6 us -> 20.1 us (0.976)
  blocking collectives: 15.3 us -> 14.9 us
    all_to_all x1, blocking collectives: 15.3 us -> 14.9 us  [body(): lax.all_to_all(send, 'wave', split_axis=0, concat_axis=0, tiled=True)]
where the time goes in v4:
time: 20.1 us; the launch traced here: 19.9 us
  blocking collectives  14.9 us (74%)
  Pallas kernels  5.01 us (25%)
    all_to_all x1, blocking collectives, body(): lax.all_to_all(send, 'wave', split_axis=0, concat_axis=0, tiled=True)  14.9 us
    pallas_call x1, Pallas kernels, body(): pl.pallas_call(lambda *refs: grid_kernel(mix, pad, *refs), out_shape=out_...  3.33 us
    pallas_call x1, Pallas kernels, body(): pl.pallas_call(lambda *refs: spectral_kernel(('wave', 'lev'), sources, mi...  1.68 us

profile of v4, /device:TPU:0, one launch (start us, length us, event | category | flops | bytes accessed | tf_op | source)
XLA Modules:
  0.0 19.9 jit_solution(3963083530481480213)
XLA Ops:
  0.0 0.0 copy-start
  0.0 3.3 %grid_side.1 = (bf16[32,3,4,128]{3,2,1,0:T(4,128)(2,1)S(1)}, bf16[16,512,128]{2,1,0:T(8,128)(2,1)S(1)}) custom-call(s32[4]{0:T(128)} %refs_0_.1, f32[3,4,4]{2,1,0:T(4,128)} %refs_1_.1, bf16[3,4,4,1536]{3,2,1,0:T(4,128)(2,1)} %refs_2_.1, bf16[4,4,1536]{2,1,0:T(4,128)(2,1)} %refs_3_.1, s32[1,512]{1,0:T(1,128)} %bitcast.2, bf16[16,512,128]{2,1,0:T(8,128)(2,1)} %refs_5_.1), custom_call_target="tpu_custom_call" | custom-call | tf_op jit(solution)/shard_map/grid_side/pallas_call | solution.py:414
  3.3 14.9 %all_to_all.5.refs_1_ = bf16[32,3,4,128]{3,2,1,0:T(4,128)(2,1)S(1)} all-to-all(bf16[32,3,4,128]{3,2,1,0:T(4,128)(2,1)S(1)} %get-tuple-element.7), channel_id=1, replica_groups=mesh['wave'=32,'lev'=1] {'wave'}, dimensions={0} | all-to-all | bytes 196608 | tf_op jit(solution)/shard_map/all_to_all | solution.py:423
  18.3 0.0 copy-done
  18.3 1.7 %spectral_side.1 = f32[1,3,4,16,2,512]{5,4,3,2,1,0:T(2,128)} custom-call(s32[1,512]{1,0:T(1,128)S(1)} %bitcast.3, bf16[32,3,4,128]{3,2,1,0:T(4,128)(2,1)S(1)} %all_to_all.5.refs_1_, bf16[16,512,128]{2,1,0:T(8,128)(2,1)S(1)} %get-tuple-element.8.refs_2_), custom_call_target="tpu_custom_call" | custom-call | tf_op jit(solution)/shard_map/spectral_side/pallas_call | solution.py:436
Async XLA Ops:
  0.0 18.3 %copy-start = (s32[512]{0:T(512)S(1)}, s32[512]{0:T(512)}, u32[]{:S(2)}) copy-start(s32[512]{0:T(512)} %param.9) | copy-start | bytes 6148

commit v5 on v4

--- a/solution.py
+++ b/solution.py
@@ -167,30 +167,24 @@
             g = grid_rows[j * pad:(j + 1) * pad, at]
             w = wind_rows[j * half_pad:(j + 1) * half_pad, at]
             g_ref[j, t] = g
-            f_ref[j, t + 1] = g * jnp.concatenate([w, w], axis=0)
+            f_ref[j, t] = g * jnp.concatenate([w, w], axis=0)
 
     lane = iota((pad, LANES), 1)
     point = within_tile(lane)
+    advected = []
     for j in range(rows):
         length = points_ref[j]
-        next_tile = length // LANES
-        next_lane = length % LANES
-        f_ref[j, 0] = pltpu.roll(
-            f_ref[j, (length - 1) // LANES + 1], LANES - 1 - (length - 1) % LANES, 1
-        )
-        f_ref[j, tiles + 1] = jnp.zeros((pad, LANES), jnp.float32)
-        f_ref[j, next_tile + 1] = jnp.where(
-            lane == next_lane, pltpu.roll(f_ref[j, 1], next_lane, 1), f_ref[j, next_tile + 1]
-        )
-    advected = []
-    for j in range(rows):
-        flux = [f_ref[j, t] for t in range(tiles + 2)]
-        ahead = [pltpu.roll(f, LANES - 1, 1) for f in flux[1:]]
-        behind = [pltpu.roll(f, 1, 1) for f in flux[:-1]]
+        last_lane = (length - 1) % LANES
+        head = pltpu.roll(f_ref[j, 0], last_lane, 1)
+        tail = pltpu.roll(f_ref[j, (length - 1) // LANES], (LANES - last_lane) % LANES, 1)
+        flux = [f_ref[j, t] for t in range(tiles)]
+        ahead = [pltpu.roll(f, LANES - 1, 1) for f in flux]
+        behind = [pltpu.roll(f, 1, 1) for f in flux]
         parts = []
         for t in range(tiles):
-            forward = jnp.where(lane == LANES - 1, ahead[t + 1], ahead[t])
-            backward = jnp.where(lane == 0, behind[t], behind[t + 1])
+            forward = jnp.where(lane == LANES - 1, ahead[(t + 1) % tiles], ahead[t])
+            forward = jnp.where(lane == length - 1 - t * LANES, head, forward)
+            backward = jnp.where(lane == 0, behind[t - 1] if t else tail, behind[t])
             parts.append((g_ref[j, t] + (forward - backward)).astype(jnp.bfloat16))
         advected.append(jnp.concatenate(parts, axis=1))
     for j in range(rows):
@@ -389,7 +383,7 @@
         pltpu.VMEM(grid_adjoint.shape, grid_adjoint.dtype),
         pltpu.VMEM(courant.shape, courant.dtype),
         pltpu.VMEM((row_count, tiles, pad, LANES), jnp.float32),
-        pltpu.VMEM((row_count, tiles + 2, pad, LANES), jnp.float32),
+        pltpu.VMEM((row_count, tiles, pad, LANES), jnp.float32),
         pltpu.VMEM((row_count, half_tiles + tiles, pad, LANES), jnp.float32),
         pltpu.VMEM((row_count, 2 * half_width, LANES), jnp.bfloat16),
         pltpu.VMEM((groups, used, LANES), jnp.float32),

time: 20.1 us -> 19.8 us (0.985)
  Pallas kernels: 5.01 us -> 4.7 us
    pallas_call x1, Pallas kernels: 3.33 us -> 3.01 us  [body(): pl.pallas_call(lambda *refs: grid_kernel(mix, pad, *refs), out_shape=out_...]
where the time goes in v5:
time: 19.8 us; the launch traced here: 19.6 us
  blocking collectives  14.9 us (75%)
  Pallas kernels  4.7 us (24%)
    all_to_all x1, blocking collectives, body(): lax.all_to_all(send, 'wave', split_axis=0, concat_axis=0, tiled=True)  14.9 us
    pallas_call x1, Pallas kernels, body(): pl.pallas_call(lambda *refs: grid_kernel(mix, pad, *refs), out_shape=out_...  3.01 us
    pallas_call x1, Pallas kernels, body(): pl.pallas_call(lambda *refs: spectral_kernel(('wave', 'lev'), sources, mi...  1.68 us

profile of v5, /device:TPU:0, one launch (start us, length us, event | category | flops | bytes accessed | tf_op | source)
XLA Modules:
  0.0 19.6 jit_solution(16255955967086870314)
XLA Ops:
  0.0 0.0 copy-start
  0.0 3.0 %grid_side.1 = (bf16[32,3,4,128]{3,2,1,0:T(4,128)(2,1)S(1)}, bf16[16,512,128]{2,1,0:T(8,128)(2,1)S(1)}) custom-call(s32[4]{0:T(128)} %refs_0_.1, f32[3,4,4]{2,1,0:T(4,128)} %refs_1_.1, bf16[3,4,4,1536]{3,2,1,0:T(4,128)(2,1)} %refs_2_.1, bf16[4,4,1536]{2,1,0:T(4,128)(2,1)} %refs_3_.1, s32[1,512]{1,0:T(1,128)} %bitcast.2, bf16[16,512,128]{2,1,0:T(8,128)(2,1)} %refs_5_.1), custom_call_target="tpu_custom_call" | custom-call | tf_op jit(solution)/shard_map/grid_side/pallas_call | solution.py:408
  3.0 14.9 %all_to_all.5.refs_1_ = bf16[32,3,4,128]{3,2,1,0:T(4,128)(2,1)S(1)} all-to-all(bf16[32,3,4,128]{3,2,1,0:T(4,128)(2,1)S(1)} %get-tuple-element.7), channel_id=1, replica_groups=mesh['wave'=32,'lev'=1] {'wave'}, dimensions={0} | all-to-all | bytes 196608 | tf_op jit(solution)/shard_map/all_to_all | solution.py:417
  17.9 0.0 copy-done
  17.9 1.7 %spectral_side.1 = f32[1,3,4,16,2,512]{5,4,3,2,1,0:T(2,128)} custom-call(s32[1,512]{1,0:T(1,128)S(1)} %bitcast.3, bf16[32,3,4,128]{3,2,1,0:T(4,128)(2,1)S(1)} %all_to_all.5.refs_1_, bf16[16,512,128]{2,1,0:T(8,128)(2,1)S(1)} %get-tuple-element.8.refs_2_), custom_call_target="tpu_custom_call" | custom-call | tf_op jit(solution)/shard_map/spectral_side/pallas_call | solution.py:430
Async XLA Ops:
  0.0 17.9 %copy-start = (s32[512]{0:T(512)S(1)}, s32[512]{0:T(512)}, u32[]{:S(2)}) copy-start(s32[512]{0:T(512)} %param.9) | copy-start | bytes 6148

commit v6 on v5

--- a/solution.py
+++ b/solution.py
@@ -187,7 +187,6 @@
             backward = jnp.where(lane == 0, behind[t - 1] if t else tail, behind[t])
             parts.append((g_ref[j, t] + (forward - backward)).astype(jnp.bfloat16))
         advected.append(jnp.concatenate(parts, axis=1))
-    for j in range(rows):
         if mix:
             mixed = jnp.dot(
                 matrix, jnp.concatenate([advected[j]] * 3, axis=0),

time: 19.8 us -> 19.8 us (level)
  no operation moved by 1% of the time
where the time goes in v6:
time: 19.8 us; the launch traced here: 19.6 us
  blocking collectives  14.9 us (75%)
  Pallas kernels  4.7 us (24%)
    all_to_all x1, blocking collectives, body(): lax.all_to_all(send, 'wave', split_axis=0, concat_axis=0, tiled=True)  14.9 us
    pallas_call x1, Pallas kernels, body(): pl.pallas_call(lambda *refs: grid_kernel(mix, pad, *refs), out_shape=out_...  3.01 us
    pallas_call x1, Pallas kernels, body(): pl.pallas_call(lambda *refs: spectral_kernel(('wave', 'lev'), sources, mi...  1.68 us

profile of v6, /device:TPU:0, one launch (start us, length us, event | category | flops | bytes accessed | tf_op | source)
XLA Modules:
  0.0 19.6 jit_solution(16255955967086870314)
XLA Ops:
  0.0 0.0 copy-start
  0.0 3.0 %grid_side.1 = (bf16[32,3,4,128]{3,2,1,0:T(4,128)(2,1)S(1)}, bf16[16,512,128]{2,1,0:T(8,128)(2,1)S(1)}) custom-call(s32[4]{0:T(128)} %refs_0_.1, f32[3,4,4]{2,1,0:T(4,128)} %refs_1_.1, bf16[3,4,4,1536]{3,2,1,0:T(4,128)(2,1)} %refs_2_.1, bf16[4,4,1536]{2,1,0:T(4,128)(2,1)} %refs_3_.1, s32[1,512]{1,0:T(1,128)} %bitcast.2, bf16[16,512,128]{2,1,0:T(8,128)(2,1)} %refs_5_.1), custom_call_target="tpu_custom_call" | custom-call | tf_op jit(solution)/shard_map/grid_side/pallas_call | solution.py:407
  3.0 14.9 %all_to_all.5.refs_1_ = bf16[32,3,4,128]{3,2,1,0:T(4,128)(2,1)S(1)} all-to-all(bf16[32,3,4,128]{3,2,1,0:T(4,128)(2,1)S(1)} %get-tuple-element.7), channel_id=1, replica_groups=mesh['wave'=32,'lev'=1] {'wave'}, dimensions={0} | all-to-all | bytes 196608 | tf_op jit(solution)/shard_map/all_to_all | solution.py:416
  17.9 0.0 copy-done
  18.0 1.7 %spectral_side.1 = f32[1,3,4,16,2,512]{5,4,3,2,1,0:T(2,128)} custom-call(s32[1,512]{1,0:T(1,128)S(1)} %bitcast.3, bf16[32,3,4,128]{3,2,1,0:T(4,128)(2,1)S(1)} %all_to_all.5.refs_1_, bf16[16,512,128]{2,1,0:T(8,128)(2,1)S(1)} %get-tuple-element.8.refs_2_), custom_call_target="tpu_custom_call" | custom-call | tf_op jit(solution)/shard_map/spectral_side/pallas_call | solution.py:429
Async XLA Ops:
  0.0 18.0 %copy-start = (s32[512]{0:T(512)S(1)}, s32[512]{0:T(512)}, u32[]{:S(2)}) copy-start(s32[512]{0:T(512)} %param.9) | copy-start | bytes 6148
